TPU v7x, 512 devices: a whole 4x4x16 slice. The times are simulated.
512 devices in a mesh: hour: 16 (over z), dom: 32 (over x, y, core).
Axes of the slice: x: 4, y: 4, z: 16, core: 2. Of those that a mesh axis runs over, the one named last changes fastest.
Arguments:
- query_matrix: bfloat16 [16, 4096, 1024], P('hour', 'dom'), may hold values from -1.6953125 to 1.6953125
- key_matrix: bfloat16 [16, 4096, 1024], P('hour', 'dom'), may hold values from -1.6953125 to 1.6953125
- value_matrix: bfloat16 [16, 4096, 1024], P('hour', 'dom'), may hold values from -6 to 6
- saved_output: bfloat16 [16, 4096, 1024], P('hour', 'dom'), may hold values from -6 to 6
- output_grad: bfloat16 [16, 4096, 1024], P('hour', 'dom'), may hold values from -16 to 16
- row_logsum: float32 [16, 16, 4096], P('hour', None, 'dom'), may hold values from 5.7 to 6.7
- key_blocks: int32 [32, 1], P('dom'), may hold values from 0 to 1, as said below
- halo_rows: int32 [32, 32, 4], replicated, may hold values from -1 to 127, as said below
Outputs:
- query_grad: bfloat16 [16, 4096, 1024], P('hour', 'dom')
- key_grad: bfloat16 [16, 4096, 1024], P('hour', 'dom')
- value_grad: bfloat16 [16, 4096, 1024], P('hour', 'dom')
Inputs may be any that keep to these rules, and one draw needn't show every extreme that they name: `key_blocks`: row d + b holds 1 distinct candidate blocks in increasing order for query block b of partition d. `halo_rows`: entry [d, p, c] is the row, within partition p, that partition d receives in slot c, or -1 for an empty slot. No partition receives from itself; from each partition the live slots come first; partition d receives 4 live rows from partition (d + 1) % 32; entry c lies in rows c * (32) to (c + 1) * 32 - 1.
All inputs are finite; a program needn't handle non-finite values.
Results may differ from a plain program's by a relative error of at most 0.0049.
Values may be sent and summed in bfloat16 or wider, within the bound.
No kernel may reach another device: no remote copies, remote signals or barrier semaphores. Data moves between devices by JAX's collectives and lax.ppermute only.
A program may use at most 64 MiB of HBM per device.

v0:
```python
import jax
import jax.numpy as jnp
from jax import lax
from jax.sharding import PartitionSpec as P

BLK = 128


def from_behind(block, axis, distance):
    devices = range(lax.axis_size(axis))
    route = [(i - distance, i) for i in devices if i - distance in devices]
    return lax.ppermute(block, axis, route)


def attend(queries, cotangent, logsum, row_delta, key_set, value_set, live_mask, head_dim):
    query_count = queries.shape[0]
    key_count = key_set.shape[0]
    head_count = logsum.shape[0]
    factor = head_dim ** (-0.5)
    query_heads = queries.reshape(query_count, head_count, head_dim)
    cot_heads = cotangent.reshape(query_count, head_count, head_dim)
    key_heads = key_set.reshape(key_count, head_count, head_dim)
    value_heads = value_set.reshape(key_count, head_count, head_dim)
    scores = (
        jnp.einsum("qhd,khd->hqk", query_heads, key_heads, preferred_element_type=jnp.float32)
        * factor
    )
    weights = jnp.where(live_mask[None, None, :], jnp.exp(scores - logsum[:, :, None]), 0.0)
    grad_weights = jnp.einsum(
        "qhd,khd->hqk", cot_heads, value_heads, preferred_element_type=jnp.float32
    )
    grad_scores = weights * (grad_weights - row_delta[:, :, None])
    weights_low = weights.astype(jnp.bfloat16)
    grad_low = grad_scores.astype(jnp.bfloat16)
    grad_values = jnp.einsum(
        "hqk,qhd->khd", weights_low, cot_heads, preferred_element_type=jnp.float32
    )
    grad_keys = (
        jnp.einsum("hqk,qhd->khd", grad_low, query_heads, preferred_element_type=jnp.float32)
        * factor
    )
    grad_query = (
        jnp.einsum("hqk,khd->qhd", grad_low, key_heads, preferred_element_type=jnp.float32) * factor
    )
    feature_width = head_count * head_dim
    return (
        grad_query.reshape(query_count, feature_width),
        grad_keys.reshape(key_count, feature_width),
        grad_values.reshape(key_count, feature_width),
    )


def on_device(
    query_matrix,
    key_matrix,
    value_matrix,
    saved_output,
    output_grad,
    row_logsum,
    key_blocks,
    halo_rows,
):
    queries = query_matrix[0]
    key_local = key_matrix[0]
    value_local = value_matrix[0]
    cotangent = output_grad[0]
    logsum = row_logsum[0]
    token_count = queries.shape[0]
    feature_width = queries.shape[1]
    head_count = logsum.shape[0]
    head_dim = feature_width // head_count
    block_count = key_blocks.shape[0]
    domains = lax.axis_size("dom")
    capacity = halo_rows.shape[2]
    halo_total = domains * capacity
    domain_index = lax.axis_index("dom")
    hour_index = lax.axis_index("hour")
    hour_total = lax.axis_size("hour")
    products = cotangent.astype(jnp.float32) * saved_output[0].astype(jnp.float32)
    row_delta = jnp.sum(products.reshape(token_count, head_count, head_dim), axis=2).T
    outgoing = lax.dynamic_index_in_dim(halo_rows, domain_index, axis=1, keepdims=False)
    send_live = outgoing >= 0
    send_index = jnp.maximum(outgoing, 0).reshape(-1)
    send_keys = jnp.take(key_local, send_index, axis=0).reshape(domains, capacity, feature_width)
    send_values = jnp.take(value_local, send_index, axis=0).reshape(
        domains, capacity, feature_width
    )
    remote_keys, remote_values = (
        lax.all_to_all(send_keys, "dom", split_axis=0, concat_axis=0, tiled=True),
        lax.all_to_all(send_values, "dom", split_axis=0, concat_axis=0, tiled=True),
    )
    incoming = lax.dynamic_index_in_dim(halo_rows, domain_index, axis=0, keepdims=False)
    pool_keys = jnp.concatenate([key_local, remote_keys.reshape(halo_total, feature_width)], axis=0)
    pool_values = jnp.concatenate(
        [value_local, remote_values.reshape(halo_total, feature_width)], axis=0
    )
    pool_live = jnp.concatenate([jnp.ones((token_count,), jnp.bool_), (incoming >= 0).reshape(-1)])
    candidates = pool_keys.shape[0] // BLK
    tile_keys = pool_keys.reshape(candidates, BLK, feature_width)
    tile_values = pool_values.reshape(candidates, BLK, feature_width)
    tile_live = pool_live.reshape(candidates, BLK)
    pool_dk = jnp.zeros((candidates, BLK, feature_width), jnp.float32)
    pool_dv = jnp.zeros((candidates, BLK, feature_width), jnp.float32)
    prev_live = jnp.full((BLK,), hour_index > 0)
    next_live = jnp.full((BLK,), hour_index < hour_total - 1)
    prev_keys, prev_values = from_behind((key_local, value_local), "hour", 1)
    next_keys, next_values = from_behind((key_local, value_local), "hour", -1)
    chosen = key_blocks[0]
    split_at = chosen.shape[0] * BLK
    key_set = jnp.concatenate(
        [
            jnp.take(tile_keys, chosen, axis=0).reshape(split_at, feature_width),
            prev_keys,
            next_keys,
        ],
        axis=0,
    )
    value_set = jnp.concatenate(
        [
            jnp.take(tile_values, chosen, axis=0).reshape(split_at, feature_width),
            prev_values,
            next_values,
        ],
        axis=0,
    )
    live_set = jnp.concatenate(
        [jnp.take(tile_live, chosen, axis=0).reshape(-1), prev_live, next_live]
    )
    grad_query, grad_k, grad_v = attend(
        queries, cotangent, logsum, row_delta, key_set, value_set, live_set, head_dim
    )
    pool_dk = pool_dk.at[chosen].add(grad_k[:split_at].reshape(-1, BLK, feature_width))
    pool_dv = pool_dv.at[chosen].add(grad_v[:split_at].reshape(-1, BLK, feature_width))
    prev_dk_parts = grad_k[split_at : split_at + BLK]
    prev_dv_parts = grad_v[split_at : split_at + BLK]
    next_dk_parts = grad_k[split_at + BLK :]
    next_dv_parts = grad_v[split_at + BLK :]
    back_prev_k, back_prev_v = from_behind((prev_dk_parts, prev_dv_parts), "hour", -1)
    back_next_k, back_next_v = from_behind((next_dk_parts, next_dv_parts), "hour", 1)
    hour_dk = back_prev_k + back_next_k
    hour_dv = back_prev_v + back_next_v
    halo_dk = pool_dk[block_count:].reshape(domains, capacity, feature_width)
    halo_dv = pool_dv[block_count:].reshape(domains, capacity, feature_width)
    returned_dk, returned_dv = (
        lax.all_to_all(
            halo_dk.astype(jnp.bfloat16), "dom", split_axis=0, concat_axis=0, tiled=True
        ).astype(halo_dk.dtype),
        lax.all_to_all(
            halo_dv.astype(jnp.bfloat16), "dom", split_axis=0, concat_axis=0, tiled=True
        ).astype(halo_dv.dtype),
    )
    weight = send_live.reshape(-1, 1).astype(jnp.float32)
    local_dk = pool_dk[:block_count].reshape(token_count, feature_width) + hour_dk
    local_dv = pool_dv[:block_count].reshape(token_count, feature_width) + hour_dv
    local_dk = local_dk.at[send_index].add(returned_dk.reshape(-1, feature_width) * weight)
    local_dv = local_dv.at[send_index].add(returned_dv.reshape(-1, feature_width) * weight)
    return (
        grad_query.astype(jnp.bfloat16)[None],
        local_dk.astype(jnp.bfloat16)[None],
        local_dv.astype(jnp.bfloat16)[None],
    )


def solution(mesh):
    in_specs = (
        P("hour", "dom", None),
        P("hour", "dom", None),
        P("hour", "dom", None),
        P("hour", "dom", None),
        P("hour", "dom", None),
        P("hour", None, "dom"),
        P("dom", None),
        P(),
    )
    out_specs = (P("hour", "dom", None), P("hour", "dom", None), P("hour", "dom", None))
    return jax.shard_map(
        on_device, mesh=mesh, in_specs=in_specs, out_specs=out_specs, check_vma=False
    )
```

profile of v0, /device:TPU:1, one launch (start us, length us, event | category | flops | bytes accessed | tf_op | source)
XLA Modules:
  0.0 123.7 jit_solution(10286836612267035874)
XLA Ops:
  2.1 5.0 %collective-permute-start = (bf16[128,1024]{1,0:T(8,128)(2,1)}, bf16[128,1024]{1,0:T(8,128)(2,1)S(1)}, u32[]{:S(2)}, u32[]{:S(2)}) collective-permute-start(bf16[128,1024]{1,0:T(8,128)(2,1)} %bitcast.62), channel_id=1, source_target_pairs={{0,32},{32,64},{64,96},{96,128},{128,160},{160,192},{192,224},{224... | collective-permute-start | bytes 786440 | tf_op jit(solution)/shard_map/ppermute | solution.py:12
  8.4 4.9 %collective-permute-start.2 = (bf16[128,1024]{1,0:T(8,128)(2,1)}, bf16[128,1024]{1,0:T(8,128)(2,1)}, u32[]{:S(2)}, u32[]{:S(2)}) collective-permute-start(bf16[128,1024]{1,0:T(8,128)(2,1)} %bitcast.66), channel_id=1, source_target_pairs={{0,32},{32,64},{64,96},{96,128},{128,160},{160,192},{192,224},{224... | collective-permute-start | bytes 786440 | tf_op jit(solution)/shard_map/ppermute | solution.py:12
  14.9 2.0 %gather_fusion.1 = bf16[128,1024]{1,0:T(8,128)(2,1)S(1)} fusion(bf16[128,1024]{1,0:T(8,128)(2,1)} %bitcast.67, s32[1024]{0:T(1024)S(1)} %pad_clamp_fusion), kind=kCustom, calls=%fused_computation.1.clone | custom fusion | bytes 524800 | tf_op jit(solution)/shard_map/jit(_take)/gather | solution.py:85
  18.8 10.3 %all-to-all-start.1 = ((bf16[32,4,1024]{2,1,0:T(4,128)(2,1)}), bf16[32,4,1024]{2,1,0:T(4,128)(2,1)S(1)}, u32[]{:S(2)}, u32[]{:S(2)}) async-start(bf16[32,4,1024]{2,1,0:T(4,128)(2,1)} %reshape.250), calls=%async_computation.1 | async-start | bytes 524288 | tf_op jit(solution)/shard_map/all_to_all | solution.py:90
  33.2 5.0 %all-to-all-done.1 = bf16[32,4,1024]{2,1,0:T(4,128)(2,1)S(1)} async-done(((bf16[32,4,1024]{2,1,0:T(4,128)(2,1)}), bf16[32,4,1024]{2,1,0:T(4,128)(2,1)S(1)}, u32[]{:S(2)}, u32[]{:S(2)}) %all-to-all-start.1) | async-done | bytes 262176 | tf_op jit(solution)/shard_map/all_to_all | solution.py:90
  38.2 3.7 %all-to-all-start = ((bf16[32,4,1024]{2,1,0:T(4,128)(2,1)}), bf16[32,4,1024]{2,1,0:T(4,128)(2,1)S(1)}, u32[]{:S(2)}, u32[]{:S(2)}) async-start(bf16[32,4,1024]{2,1,0:T(4,128)(2,1)} %reshape.246), calls=%async_computation | async-start | bytes 524288 | tf_op jit(solution)/shard_map/all_to_all | solution.py:89
  42.1 8.9 %all-to-all-done = bf16[32,4,1024]{2,1,0:T(4,128)(2,1)S(1)} async-done(((bf16[32,4,1024]{2,1,0:T(4,128)(2,1)}), bf16[32,4,1024]{2,1,0:T(4,128)(2,1)S(1)}, u32[]{:S(2)}, u32[]{:S(2)}) %all-to-all-start) | async-done | bytes 262176 | tf_op jit(solution)/shard_map/all_to_all | solution.py:89
  54.7 1.8 %fusion.23 = f32[16,384,128]{2,1,0:T(8,128)S(1)} fusion(bf16[128,16,64]{0,2,1:T(8,128)(2,1)} %bitcast.72, bf16[128,16,64]{0,2,1:T(8,128)(2,1)} %bitcast.84, bf16[128,16,64]{0,2,1:T(8,128)(2,1)} %bitcast.86, bf16[128,16,64]{0,2,1:T(8,128)(2,1)} %bitcast.82), kind=kOutput, calls=%fused_computation.38 | convolution fusion | flops 103022592 | bytes 4194304 | tf_op jit(solution)/shard_map/qhd,khd->hqk/dot_general | solution.py:25
  56.5 1.8 %copy.36 = bf16[128,1024]{0,1:T(8,128)(2,1)} copy(bf16[128,1024]{1,0:T(8,128)(2,1)} %collective-permute-done.3) | data formatting | bytes 524288 | tf_op jit(solution)/shard_map/ppermute | solution.py:12
  58.3 2.1 %fusion.7 = f32[384,16,64]{0,2,1:T(8,128)} fusion(bf16[128,16,64]{0,2,1:T(8,128)(2,1)S(1)} %bitcast.70, f32[16,384,128]{2,1,0:T(8,128)S(1)} %fusion.23, f32[16,128]{1,0:T(8,128)S(1)} %bitcast.93, pred[384]{0:T(512)(128)(4,1)S(1)} %pad_add_fusion), kind=kOutput, calls=%fused_computation.13 | convolution fusion | flops 103809024 | bytes 4989312 | tf_op jit(solution)/shard_map/hqk,qhd->khd/dot_general | solution.py:35
  60.4 1.8 %copy.35 = bf16[128,1024]{0,1:T(8,128)(2,1)} copy(bf16[128,1024]{1,0:T(8,128)(2,1)} %collective-permute-done.2) | data formatting | bytes 524288 | tf_op jit(solution)/shard_map/ppermute | solution.py:12
  62.2 2.3 %multiply_convert_fusion = bf16[16,384,128]{2,1,0:T(8,128)(2,1)S(1)} fusion(f32[16,384,128]{2,1,0:T(8,128)S(1)} %fusion.23, bf16[128,16,64]{0,2,1:T(8,128)(2,1)S(1)} %bitcast.71, f32[16,128]{1,0:T(8,128)S(1)} %bitcast.95, f32[16,128]{1,0:T(8,128)S(1)} %bitcast.94, pred[384]{0:T(512)(128)(4,1)S(1)} %pad_add_fusion, bf16[128,16,64]{0,2,1:T(8,128)(2,1)} %bitcast.90, ...), kind=kOutput, calls=%fused_computation.4 | convolution fusion | flops 107741184 | bytes 5783936 | tf_op jit(solution)/shard_map/qhd,khd->hqk/dot_general | solution.py:29
  70.1 4.8 %collective-permute-start.5 = (f32[128,1024]{1,0:T(8,128)}, f32[128,1024]{1,0:T(8,128)}, u32[]{:S(2)}, u32[]{:S(2)}) collective-permute-start(f32[128,1024]{1,0:T(8,128)} %copy.41), channel_id=1, source_target_pairs={{0,32},{32,64},{64,96},{96,128},{128,160},{160,192},{192,224},{224... | collective-permute-start | bytes 1572872 | tf_op jit(solution)/shard_map/ppermute | solution.py:12
  75.9 4.9 %all-to-all-start.2 = ((bf16[32,4,1024]{2,1,0:T(4,128)(2,1)}), bf16[32,4,1024]{2,1,0:T(4,128)(2,1)}, u32[]{:S(2)}, u32[]{:S(2)}) async-start(bf16[32,4,1024]{2,1,0:T(4,128)(2,1)} %convert_element_type.75), calls=%async_computation.2 | async-start | bytes 524288 | tf_op jit(solution)/shard_map/all_to_all | solution.py:145
  80.8 1.9 %fusion.32 = (f32[128,16,64]{0,2,1:T(8,128)S(1)}, f32[128,16,64]{0,2,1:T(8,128)}, f32[128,16,64]{0,2,1:T(8,128)}) fusion(f32[384,16,64]{0,2,1:T(8,128)S(1)} %copy-done.2, pred[]{:T(512)} %and_reduce_fusion), kind=kLoop, calls=%fused_computation.67 | loop fusion | flops 131072 | bytes 3145729 | tf_op jit(solution)/shard_map/slice | solution.py:137
  83.9 2.1 %copy.43 = f32[128,1024]{1,0:T(8,128)} copy(f32[128,1024]{0,1:T(8,128)} %bitcast.76) | data formatting | bytes 1048576 | tf_op jit(solution)/shard_map/slice | solution.py:135
  88.3 4.8 %collective-permute-start.7 = (f32[128,1024]{1,0:T(8,128)}, f32[128,1024]{1,0:T(8,128)}, u32[]{:S(2)}, u32[]{:S(2)}) collective-permute-start(f32[128,1024]{1,0:T(8,128)} %copy.44), channel_id=1, source_target_pairs={{0,32},{32,64},{64,96},{96,128},{128,160},{160,192},{192,224},{224... | collective-permute-start | bytes 1572872 | tf_op jit(solution)/shard_map/ppermute | solution.py:12
  94.2 8.1 %all-to-all-start.3 = ((bf16[32,4,1024]{2,1,0:T(4,128)(2,1)}), bf16[32,4,1024]{2,1,0:T(4,128)(2,1)}, u32[]{:S(2)}, u32[]{:S(2)}) async-start(bf16[32,4,1024]{2,1,0:T(4,128)(2,1)} %convert_element_type.80), calls=%async_computation.3 | async-start | bytes 524288 | tf_op jit(solution)/shard_map/all_to_all | solution.py:148
  102.4 1.8 %fusion.10 = bf16[16,64,128]{2,1,0:T(8,128)(2,1)S(1)} fusion(bf16[16,384,128]{2,1,0:T(8,128)(2,1)} %copy-done.4, bf16[128,16,64]{0,2,1:T(8,128)(2,1)S(1)} %bitcast.85, bf16[128,16,64]{0,2,1:T(8,128)(2,1)S(1)} %bitcast.87, bf16[128,16,64]{0,2,1:T(8,128)(2,1)S(1)} %bitcast.83), kind=kOutput, calls=%fused_computation.15 | convolution fusion | flops 103284736 | bytes 2621440 | tf_op jit(solution)/shard_map/hqk,khd->qhd/dot_general | solution.py:43
  106.1 5.3 %all-to-all-done.3 = bf16[32,4,1024]{2,1,0:T(4,128)(2,1)} async-done(((bf16[32,4,1024]{2,1,0:T(4,128)(2,1)}), bf16[32,4,1024]{2,1,0:T(4,128)(2,1)}, u32[]{:S(2)}, u32[]{:S(2)}) %all-to-all-start.3) | async-done | bytes 262176 | tf_op jit(solution)/shard_map/all_to_all | solution.py:148
  112.4 2.1 %fusion.17 = f32[128,1024]{1,0:T(8,128)} fusion(f32[2,128,1024]{2,1,0:T(8,128)S(1)} %constant_dynamic-update-slice_fusion.1, f32[128,1024]{1,0:T(8,128)} %collective-permute-done.4, f32[128,1024]{1,0:T(8,128)} %collective-permute-done.5), kind=kLoop, calls=%fused_computation.28 | loop fusion | flops 262144 | bytes 2097152 | tf_op jit(solution)/shard_map/add | solution.py:153
  114.4 3.5 %scatter_custom_fusion = f32[128,1024]{1,0:T(8,128)} fusion(f32[128,1024]{1,0:T(8,128)} %fusion.17, s32[128]{0:T(128)S(1)} %max.18, f32[128,1024]{1,0:T(8,128)S(1)} %reshape.306, f32[128]{0:T(128)S(1)} %reshape.307), kind=kCustom, calls=%fused_computation.36 | custom fusion | flops 262144 | bytes 1049088 | tf_op jit(solution)/shard_map/scatter-add | solution.py:155
  117.9 1.8 %convert_bitcast_fusion.1 = bf16[1,128,1024]{2,1,0:T(8,128)(2,1)} fusion(f32[128,1024]{1,0:T(8,128)} %scatter_custom_fusion), kind=kLoop, calls=%fused_computation.40 | loop fusion | flops 131072 | bytes 786432 | tf_op jit(solution)/shard_map/broadcast_in_dim | solution.py:159
  121.0 1.9 %scatter_custom_fusion.1 = f32[128,1024]{1,0:T(8,128)S(1)} fusion(f32[128,1024]{1,0:T(8,128)S(1)} %fusion.16, s32[128]{0:T(128)S(1)} %max.18, f32[128,1024]{1,0:T(8,128)S(1)} %reshape.309, f32[128]{0:T(128)S(1)} %reshape.307), kind=kCustom, calls=%fused_computation.34 | custom fusion | flops 262144 | bytes 1049088 | tf_op jit(solution)/shard_map/scatter-add | solution.py:156
  (96 shorter events, 29.3 us)
Async XLA Ops:
  0.6 16.3 %copy-start = (bf16[1,128,1024]{2,1,0:T(8,128)(2,1)S(1)}, bf16[1,128,1024]{2,1,0:T(8,128)(2,1)}, u32[]{:S(2)}) copy-start(bf16[1,128,1024]{2,1,0:T(8,128)(2,1)} %param.17) | copy-start | bytes 786436
  0.6 52.4 %collective-permute-start.1 = (bf16[128,1024]{1,0:T(8,128)(2,1)}, bf16[128,1024]{1,0:T(8,128)(2,1)S(1)}, u32[]{:S(2)}, u32[]{:S(2)}) collective-permute-start(bf16[128,1024]{1,0:T(8,128)(2,1)} %bitcast.61), channel_id=1, source_target_pairs={{32,0},{64,32},{96,64},{128,96},{160,128},{192,160},{224,192},{256... | collective-permute-start | bytes 786440 | tf_op jit(solution)/shard_map/ppermute | solution.py:12
  2.1 51.8 %collective-permute-start = (bf16[128,1024]{1,0:T(8,128)(2,1)}, bf16[128,1024]{1,0:T(8,128)(2,1)S(1)}, u32[]{:S(2)}, u32[]{:S(2)}) collective-permute-start(bf16[128,1024]{1,0:T(8,128)(2,1)} %bitcast.62), channel_id=1, source_target_pairs={{0,32},{32,64},{64,96},{96,128},{128,160},{160,192},{192,224},{224... | collective-permute-start | bytes 786440 | tf_op jit(solution)/shard_map/ppermute | solution.py:12
  7.1 49.4 %collective-permute-start.3 = (bf16[128,1024]{1,0:T(8,128)(2,1)}, bf16[128,1024]{1,0:T(8,128)(2,1)}, u32[]{:S(2)}, u32[]{:S(2)}) collective-permute-start(bf16[128,1024]{1,0:T(8,128)(2,1)} %bitcast.65), channel_id=1, source_target_pairs={{32,0},{64,32},{96,64},{128,96},{160,128},{192,160},{224,192},{256... | collective-permute-start | bytes 786440 | tf_op jit(solution)/shard_map/ppermute | solution.py:12
  8.4 52.0 %collective-permute-start.2 = (bf16[128,1024]{1,0:T(8,128)(2,1)}, bf16[128,1024]{1,0:T(8,128)(2,1)}, u32[]{:S(2)}, u32[]{:S(2)}) collective-permute-start(bf16[128,1024]{1,0:T(8,128)(2,1)} %bitcast.66), channel_id=1, source_target_pairs={{0,32},{32,64},{64,96},{96,128},{128,160},{160,192},{192,224},{224... | collective-permute-start | bytes 786440 | tf_op jit(solution)/shard_map/ppermute | solution.py:12
  17.8 11.3 %copy-start.8 = (s32[32,32,4]{1,2,0:T(4,128)S(1)}, s32[32,32,4]{1,2,0:T(4,128)}, u32[]{:S(2)}) copy-start(s32[32,32,4]{1,2,0:T(4,128)} %param.23) | copy-start | bytes 49156
  17.8 12.2 %copy-start.9 = (bf16[1,128,1024]{2,1,0:T(8,128)(2,1)S(1)}, bf16[1,128,1024]{2,1,0:T(8,128)(2,1)}, u32[]{:S(2)}) copy-start(bf16[1,128,1024]{2,1,0:T(8,128)(2,1)} %param.16) | copy-start | bytes 786436
  17.9 13.9 %copy-start.10 = (bf16[1,128,1024]{2,1,0:T(8,128)(2,1)S(1)}, bf16[1,128,1024]{2,1,0:T(8,128)(2,1)}, u32[]{:S(2)}) copy-start(bf16[1,128,1024]{2,1,0:T(8,128)(2,1)} %param.20) | copy-start | bytes 786436
  18.0 13.9 %copy-start.11 = (bf16[1,128,1024]{2,1,0:T(8,128)(2,1)S(1)}, bf16[1,128,1024]{2,1,0:T(8,128)(2,1)}, u32[]{:S(2)}) copy-start(bf16[1,128,1024]{2,1,0:T(8,128)(2,1)} %param.19) | copy-start | bytes 786436
  18.0 14.4 %copy-start.13 = (s32[3]{0:T(128)S(1)}, s32[3]{0:T(128)}, u32[]{:S(2)}) copy-start(s32[3]{0:T(128)} %constant.112.clone.1) | copy-start | bytes 40
  18.8 19.4 %all-to-all-start.1 = ((bf16[32,4,1024]{2,1,0:T(4,128)(2,1)}), bf16[32,4,1024]{2,1,0:T(4,128)(2,1)S(1)}, u32[]{:S(2)}, u32[]{:S(2)}) async-start(bf16[32,4,1024]{2,1,0:T(4,128)(2,1)} %reshape.250), calls=%async_computation.1 | async-start | bytes 524288 | tf_op jit(solution)/shard_map/all_to_all | solution.py:90
  30.9 11.2 %copy-start.1 = (bf16[1,128,1024]{2,1,0:T(8,128)(2,1)S(1)}, bf16[1,128,1024]{2,1,0:T(8,128)(2,1)}, u32[]{:S(2)}) copy-start(bf16[1,128,1024]{2,1,0:T(8,128)(2,1)} %param.18) | copy-start | bytes 786436
  38.2 12.8 %all-to-all-start = ((bf16[32,4,1024]{2,1,0:T(4,128)(2,1)}), bf16[32,4,1024]{2,1,0:T(4,128)(2,1)S(1)}, u32[]{:S(2)}, u32[]{:S(2)}) async-start(bf16[32,4,1024]{2,1,0:T(4,128)(2,1)} %reshape.246), calls=%async_computation | async-start | bytes 524288 | tf_op jit(solution)/shard_map/all_to_all | solution.py:89
  54.7 3.6 %copy-start.12 = (f32[1,16,128]{2,1,0:T(8,128)S(1)}, f32[1,16,128]{2,1,0:T(8,128)}, u32[]{:S(2)}) copy-start(f32[1,16,128]{2,1,0:T(8,128)} %param.21) | copy-start | bytes 24580
  67.8 44.6 %collective-permute-start.4 = (f32[128,1024]{1,0:T(8,128)}, f32[128,1024]{1,0:T(8,128)}, u32[]{:S(2)}, u32[]{:S(2)}) collective-permute-start(f32[128,1024]{1,0:T(8,128)} %copy.40), channel_id=1, source_target_pairs={{32,0},{64,32},{96,64},{128,96},{160,128},{192,160},{224,192},{256... | collective-permute-start | bytes 1572872 | tf_op jit(solution)/shard_map/ppermute | solution.py:12
  70.1 42.3 %collective-permute-start.5 = (f32[128,1024]{1,0:T(8,128)}, f32[128,1024]{1,0:T(8,128)}, u32[]{:S(2)}, u32[]{:S(2)}) collective-permute-start(f32[128,1024]{1,0:T(8,128)} %copy.41), channel_id=1, source_target_pairs={{0,32},{32,64},{64,96},{96,128},{128,160},{160,192},{192,224},{224... | collective-permute-start | bytes 1572872 | tf_op jit(solution)/shard_map/ppermute | solution.py:12
  75.0 5.8 %copy-start.2 = (f32[384,16,64]{0,2,1:T(8,128)S(1)}, f32[384,16,64]{0,2,1:T(8,128)}, u32[]{:S(2)}) copy-start(f32[384,16,64]{0,2,1:T(8,128)} %fusion.7) | copy-start | bytes 4718596
  75.9 18.3 %all-to-all-start.2 = ((bf16[32,4,1024]{2,1,0:T(4,128)(2,1)}), bf16[32,4,1024]{2,1,0:T(4,128)(2,1)}, u32[]{:S(2)}, u32[]{:S(2)}) async-start(bf16[32,4,1024]{2,1,0:T(4,128)(2,1)} %convert_element_type.75), calls=%async_computation.2 | async-start | bytes 524288 | tf_op jit(solution)/shard_map/all_to_all | solution.py:145
  86.0 33.7 %collective-permute-start.6 = (f32[128,1024]{1,0:T(8,128)}, f32[128,1024]{1,0:T(8,128)}, u32[]{:S(2)}, u32[]{:S(2)}) collective-permute-start(f32[128,1024]{1,0:T(8,128)} %copy.43), channel_id=1, source_target_pairs={{32,0},{64,32},{96,64},{128,96},{160,128},{192,160},{224,192},{256... | collective-permute-start | bytes 1572872 | tf_op jit(solution)/shard_map/ppermute | solution.py:12
  88.3 31.4 %collective-permute-start.7 = (f32[128,1024]{1,0:T(8,128)}, f32[128,1024]{1,0:T(8,128)}, u32[]{:S(2)}, u32[]{:S(2)}) collective-permute-start(f32[128,1024]{1,0:T(8,128)} %copy.44), channel_id=1, source_target_pairs={{0,32},{32,64},{64,96},{96,128},{128,160},{160,192},{192,224},{224... | collective-permute-start | bytes 1572872 | tf_op jit(solution)/shard_map/ppermute | solution.py:12
  93.2 9.1 %copy-start.5 = (bf16[1,128,1024]{1,2,0:T(8,128)(2,1)S(1)}, bf16[1,128,1024]{1,2,0:T(8,128)(2,1)}, u32[]{:S(2)}) copy-start(bf16[1,128,1024]{1,2,0:T(8,128)(2,1)} %broadcast_select_fusion.3) | copy-start | bytes 786436
  93.2 9.1 %copy-start.6 = (bf16[128,1024]{0,1:T(8,128)(2,1)S(1)}, bf16[128,1024]{0,1:T(8,128)(2,1)}, u32[]{:S(2)}) copy-start(bf16[128,1024]{0,1:T(8,128)(2,1)} %copy.31) | copy-start | bytes 786436
  93.3 9.1 %copy-start.7 = (bf16[128,1024]{0,1:T(8,128)(2,1)S(1)}, bf16[128,1024]{0,1:T(8,128)(2,1)}, u32[]{:S(2)}) copy-start(bf16[128,1024]{0,1:T(8,128)(2,1)} %copy.30) | copy-start | bytes 786436
  94.2 17.1 %all-to-all-start.3 = ((bf16[32,4,1024]{2,1,0:T(4,128)(2,1)}), bf16[32,4,1024]{2,1,0:T(4,128)(2,1)}, u32[]{:S(2)}, u32[]{:S(2)}) async-start(bf16[32,4,1024]{2,1,0:T(4,128)(2,1)} %convert_element_type.80), calls=%async_computation.3 | async-start | bytes 524288 | tf_op jit(solution)/shard_map/all_to_all | solution.py:148
  (2 other events, 3.5 us)
where the time goes:
time: 125 us; the launch traced here: 124 us
  starting transfers between devices  51.8 us (41%)
  local copies, waits for them, and re-layouts  23.7 us (19%)
  waiting for transfers between devices  19.1 us (15%)
  other arithmetic  18.4 us (15%)
  matrix products  8.86 us (7%)
  between operations  1.85 us (1%)
    ppermute x8, starting transfers between devices, from_behind(): return lax.ppermute(block, axis, route)  24.7 us
    all_to_all x1, starting transfers between devices, on_device(): lax.all_to_all(send_values, 'dom', split_axis=0, concat_axis=0, tiled=True)  10.3 us
    all_to_all x1, waiting for transfers between devices, on_device(): lax.all_to_all(send_keys, 'dom', split_axis=0, concat_axis=0, tiled=True)  8.85 us
    all_to_all x1, starting transfers between devices, on_device(): lax.all_to_all(halo_dv.astype(jnp.bfloat16), 'dom', split_axis=0, concat_...  8.12 us
    all_to_all x1, waiting for transfers between devices, on_device(): lax.all_to_all(halo_dv.astype(jnp.bfloat16), 'dom', split_axis=0, concat_...  5.29 us
    ppermute x4, local copies, waits for them, and re-layouts, from_behind(): return lax.ppermute(block, axis, route)  5.26 us
    all_to_all x1, waiting for transfers between devices, on_device(): lax.all_to_all(send_values, 'dom', split_axis=0, concat_axis=0, tiled=True)  4.98 us
    all_to_all x1, starting transfers between devices, on_device(): lax.all_to_all(halo_dk.astype(jnp.bfloat16), 'dom', split_axis=0, concat_...  4.91 us
  transfers between devices with their start and end apart: 12, of which 3 were waited for; matrix products, arithmetic and copies ran while one was open for 32% of the time, Pallas kernels for 0%

commit v1 on v0

v1 whole, which is shorter than its diff:
```python
import functools
import math

import jax
import jax.numpy as jnp
from jax import lax
from jax.experimental import pallas as pl
from jax.experimental.pallas import tpu as pltpu
from jax.sharding import PartitionSpec as P

BF = jnp.bfloat16
F32 = jnp.float32
LANES = 128
VMEM_LIMIT = 24 << 20


def dot(a, b):
    return lax.dot_general(a, b, (((1,), (0,)), ((), ())), preferred_element_type=F32)


def dot_nt(a, b):
    return lax.dot_general(a, b, (((1,), (1,)), ((), ())), preferred_element_type=F32)


def dot_tn(a, b):
    return lax.dot_general(a, b, (((0,), (0,)), ((), ())), preferred_element_type=F32)


def iota(shape, dim):
    return lax.broadcasted_iota(jnp.int32, shape, dim)


def one_where(mask):
    return jnp.where(mask, 1.0, 0.0).astype(BF)


def split3(x):
    hi = x.astype(BF)
    rest = x - hi.astype(F32)
    mid = rest.astype(BF)
    return hi, mid, (rest - mid.astype(F32)).astype(BF)


def fetch(copies):
    for copy in copies:
        copy.start()
    return copies


def picks(halo, me, cap, slots, tokens, by_slot):
    rows = halo.astype(F32)
    twice = jnp.concatenate([rows, rows], axis=1)
    table = twice.reshape(slots, twice.shape[2]).astype(BF)
    owners = table.shape[1]
    shape = (slots, tokens) if by_slot else (tokens, slots)
    if by_slot:
        wanted = dot(table, one_where(iota((owners, tokens), 0) == me))
    else:
        wanted = dot_nt(one_where(iota((tokens, owners), 1) == me), table)
    slot_dim = 0 if by_slot else 1
    hit = wanted.astype(jnp.int32) == iota(shape, 1 - slot_dim)
    is_key = (iota(shape, slot_dim) % (2 * cap)) < cap
    both = [one_where(hit & is_key), one_where(hit & ~is_key)]
    return jnp.concatenate(both, axis=1 - slot_dim)


def front_kernel(
    me_ref,
    halo_hbm,
    query_hbm,
    key_hbm,
    value_hbm,
    cot_hbm,
    saved_hbm,
    logsum_hbm,
    pack_ref,
    send_hbm,
    halo_ref,
    saved_ref,
    logsum_ref,
    send_ref,
    sems,
):
    tokens, width = query_hbm.shape
    heads = logsum_hbm.shape[0]
    head_dim = width // heads
    slots = send_ref.shape[0]
    cap = halo_hbm.shape[1]
    pieces = [
        (halo_hbm, halo_ref),
        (key_hbm, pack_ref.at[:, width : 2 * width]),
        (value_hbm, pack_ref.at[:, 2 * width : 3 * width]),
        (cot_hbm, pack_ref.at[:, 3 * width : 4 * width]),
        (saved_hbm, saved_ref),
        (logsum_hbm, logsum_ref),
        (query_hbm, pack_ref.at[:, :width]),
    ]
    copies = fetch(
        [pltpu.make_async_copy(a, b, sems.at[i]) for i, (a, b) in enumerate(pieces)]
    )
    copies[0].wait()
    pick = picks(halo_ref[...], me_ref[0], cap, slots, tokens, True)
    copies[1].wait()
    copies[2].wait()
    both = jnp.concatenate(
        [pack_ref[:, width : 2 * width], pack_ref[:, 2 * width : 3 * width]], axis=0
    )
    send_ref[...] = dot(pick, both).astype(BF)
    out = pltpu.make_async_copy(send_ref, send_hbm, sems.at[len(pieces)])
    out.start()
    for copy in copies[3:]:
        copy.wait()
    product = pack_ref[:, 3 * width : 4 * width].astype(F32) * saved_ref[...].astype(F32)
    high = product.astype(BF)
    low = (product - high.astype(F32)).astype(BF)
    member = one_where(iota((heads, width), 1) // head_dim == iota((heads, width), 0))
    delta = dot_nt(member, high) + dot_nt(member, low)
    parts = [p.astype(F32) for p in split3(logsum_ref[...]) + split3(delta)]
    parts.append(jnp.zeros((LANES - 6 * heads, tokens), F32))
    pack_ref[:, 4 * width :] = jnp.concatenate(parts, axis=0).T.astype(BF)
    out.wait()


def extra_mask(head, heads, first):
    lane = iota((16, LANES), 1)
    inside = (lane >= first) & (lane < first + 3 * heads)
    return one_where(inside & (lane % heads == head))


def rows_of(pattern, tokens):
    return jnp.concatenate([pattern] * (tokens // pattern.shape[0]), axis=0)


def half_masks(tokens, head_dim):
    low = one_where(iota((16, LANES), 1) < head_dim)
    high = one_where(iota((16, LANES), 1) >= head_dim)
    return rows_of(low, tokens), rows_of(high, tokens)


def weights_of(rows, row_extra, columns, column_extra, scale):
    left = jnp.concatenate([rows, row_extra], axis=1)
    right = jnp.concatenate([columns, column_extra], axis=1)
    return dot_nt(left, right)


def key_side(keys, values, two_query, two_cot, two_logsum, two_delta, constants, scale):
    minus_inverse, minus_one = constants
    score = weights_of(keys, minus_inverse, two_query, two_logsum, scale)
    grad = weights_of(values, minus_one, two_cot, two_delta, scale)
    weight = jnp.exp2(score * (scale * math.log2(math.e)))
    grad_low = (weight * grad).astype(BF)
    value_grad = dot(weight.astype(BF), two_cot)
    key_grad = dot(grad_low, two_query)
    return key_grad, value_grad, grad_low


def two_heads(block, masks):
    return jnp.concatenate([block * masks[0], block * masks[1]], axis=0)


def two_extras(extra, pair, heads, first):
    tokens = extra.shape[0]
    return jnp.concatenate(
        [extra * rows_of(extra_mask(2 * pair + i, heads, first), tokens) for i in (0, 1)], axis=0
    )


def spread(slots, cap, by_slot):
    half = slots // 2
    shape = (slots, half) if by_slot else (half, slots)
    row, column = iota(shape, 0 if by_slot else 1), iota(shape, 1 if by_slot else 0)
    owner, place = row // (2 * cap), row % (2 * cap)
    keys = one_where((place < cap) & (column == owner * cap + place))
    values = one_where((place >= cap) & (column == owner * cap + place - cap))
    return jnp.concatenate([keys, values], axis=1 if by_slot else 0)


def halo_kernel(
    heads, cap, block_ref, pack_ref, recv_ref, part_hbm, back_hbm, pool, part, back, sems
):
    tokens = pack_ref.shape[0]
    slots, width = recv_ref.shape
    head_dim = width // heads
    scale = head_dim**-0.5
    local = block_ref[0] == 0

    @pl.when(local)
    def _():
        pool[:tokens] = pack_ref[:, width : 2 * width]
        pool[tokens:] = pack_ref[:, 2 * width : 3 * width]

    @pl.when(jnp.logical_not(local))
    def _():
        pool[...] = dot(spread(slots, cap, False), recv_ref[...]).astype(BF)

    masks = half_masks(tokens, head_dim)
    extra = pack_ref[:, 4 * width :]
    constants = (
        jnp.full((tokens, LANES), -1.0 / scale, BF),
        jnp.full((tokens, LANES), -1.0, BF),
    )
    low_lane = iota((tokens, LANES), 1) < head_dim
    layout = spread(slots, cap, True)
    to_own = jnp.where(local, 1.0, 0.0)
    to_halo = 1.0 - to_own
    outs = []
    for quad in range(heads // 4):
        both = []
        for pair in (2 * quad, 2 * quad + 1):
            at = pair * LANES
            keys = pool[:tokens, at : at + LANES]
            values = pool[tokens:, at : at + LANES]
            two_query = two_heads(pack_ref[:, at : at + LANES], masks)
            two_cot = two_heads(pack_ref[:, 3 * width + at : 3 * width + at + LANES], masks)
            key_grad, value_grad, grad_low = key_side(
                keys,
                values,
                two_query,
                two_cot,
                two_extras(extra, pair, heads, 0),
                two_extras(extra, pair, heads, 3 * heads),
                constants,
                scale,
            )
            key_grad = key_grad * scale
            query_grad = dot_tn(grad_low, keys)
            part[:tokens, at : at + LANES] = jnp.where(
                low_lane, query_grad[:tokens], query_grad[tokens:]
            )
            part[tokens : 2 * tokens, at : at + LANES] = key_grad * to_own
            part[2 * tokens :, at : at + LANES] = value_grad * to_own
            both.append(
                jnp.concatenate([key_grad * to_halo, value_grad * to_halo], axis=0).astype(BF)
            )
        lanes = slice(2 * quad * LANES, 2 * (quad + 1) * LANES)
        back[:, lanes] = dot(layout, jnp.concatenate(both, axis=1)).astype(BF)
        outs += fetch(
            [
                pltpu.make_async_copy(part.at[:, lanes], part_hbm.at[:, lanes], sems.at[2 * quad]),
                pltpu.make_async_copy(
                    back.at[:, lanes], back_hbm.at[:, lanes], sems.at[2 * quad + 1]
                ),
            ]
        )
    for copy in outs:
        copy.wait()


def hours_kernel(
    heads,
    me_ref,
    halo_hbm,
    pack_ref,
    first_hbm,
    second_hbm,
    part_hbm,
    query_hbm,
    total_ref,
    place_ref,
    halo_ref,
    first_ref,
    second_ref,
    part_ref,
    query_ref,
    sems,
):
    tokens, width = query_hbm.shape
    head_dim = width // heads
    scale = head_dim**-0.5
    pieces = [
        (halo_hbm, halo_ref),
        (part_hbm, part_ref),
        (first_hbm, first_ref),
        (second_hbm, second_ref),
    ]
    copies = fetch(
        [pltpu.make_async_copy(a, b, sems.at[i]) for i, (a, b) in enumerate(pieces)]
    )
    copies[0].wait()
    cap = halo_ref.shape[1]
    slots = place_ref.shape[1]
    place_ref[...] = picks(halo_ref[...], me_ref[0], cap, slots, tokens, False)
    for copy in copies[1:]:
        copy.wait()
    masks = half_masks(tokens, head_dim)
    own_extra = pack_ref[:, 4 * width :]
    constants = (
        jnp.full((tokens, LANES), -1.0 / scale, BF),
        jnp.full((tokens, LANES), -1.0, BF),
    )
    outs = []
    for pair in range(heads // 2):
        at = pair * LANES
        lanes = slice(at, at + LANES)
        own = [pack_ref[:, i * width + at : i * width + at + LANES] for i in range(4)]
        query_total = part_ref[:tokens, lanes]
        key_total = jnp.zeros((tokens, LANES), F32)
        value_total = part_ref[2 * tokens :, lanes]
        logsum_lanes, delta_lanes = (
            jnp.concatenate(
                [rows_of(extra_mask(2 * pair + i, heads, at_lane) * BF(by), tokens) for i in (0, 1)],
                axis=0,
            )
            for at_lane, by in ((0, -1.0 / scale), (3 * heads, -1.0))
        )
        for other_ref in (first_ref, second_ref):
            other = [other_ref[:, i * width + at : i * width + at + LANES] for i in range(4)]
            two_query, two_key, two_value, two_cot = (two_heads(block, masks) for block in other)
            other_extra = other_ref[:, 4 * width :]
            key_grad, value_grad, _ = key_side(
                own[1],
                own[2],
                two_query,
                two_cot,
                two_extras(other_extra, pair, heads, 0),
                two_extras(other_extra, pair, heads, 3 * heads),
                constants,
                scale,
            )
            key_total += key_grad
            value_total += value_grad
            score = weights_of(own[0], own_extra, two_key, logsum_lanes, scale)
            grad = weights_of(own[3], own_extra, two_value, delta_lanes, scale)
            weight = jnp.exp2(score * (scale * math.log2(math.e)))
            query_total += dot((weight * grad).astype(BF), two_key)
        query_ref[:, lanes] = (query_total * scale).astype(BF)
        total_ref[:tokens, lanes] = part_ref[tokens : 2 * tokens, lanes] + key_total * scale
        total_ref[tokens:, lanes] = value_total
        if pair % 4 == 3:
            done = slice((pair - 3) * LANES, (pair + 1) * LANES)
            outs += fetch(
                [
                    pltpu.make_async_copy(
                        query_ref.at[:, done],
                        query_hbm.at[:, done],
                        sems.at[len(pieces) + pair // 4],
                    )
                ]
            )
    for copy in outs:
        copy.wait()


def scatter_kernel(place_ref, returned_ref, total_ref, key_hbm, value_hbm, out_ref, sems):
    tokens, width = key_hbm.shape
    outs = []
    chunk = 2 * LANES
    for i in range(width // chunk):
        lanes = slice(i * chunk, (i + 1) * chunk)
        out_ref[:, lanes] = (
            total_ref[:, lanes] + dot(place_ref[...], returned_ref[:, lanes])
        ).astype(BF)
        outs += fetch(
            [
                pltpu.make_async_copy(
                    out_ref.at[j * tokens : (j + 1) * tokens, lanes],
                    hbm.at[:, lanes],
                    sems.at[2 * i + j],
                )
                for j, hbm in enumerate((key_hbm, value_hbm))
            ]
        )
    for copy in outs:
        copy.wait()


SMEM, VMEM, HBM = pltpu.SMEM, pltpu.VMEM, pltpu.HBM


def call(kernel, ins, outs, cost, scratch, sems, name):
    run = pl.pallas_call(
        kernel,
        out_shape=tuple(space(shape, kind) for shape, kind, space in outs),
        in_specs=[pl.BlockSpec(memory_space=space) for space in ins],
        out_specs=tuple(pl.BlockSpec(memory_space=space) for _, _, space in outs),
        scratch_shapes=[pltpu.VMEM(*s) for s in scratch] + [pltpu.SemaphoreType.DMA((sems,))],
        compiler_params=pltpu.CompilerParams(vmem_limit_bytes=VMEM_LIMIT),
        cost_estimate=pl.CostEstimate(flops=cost[0], bytes_accessed=cost[1], transcendentals=0),
        name=name,
    )

    def placed(*args):
        return run(
            *(
                pltpu.with_memory_space_constraint(x, space) if space is HBM else x
                for x, space in zip(args, ins, strict=True)
            )
        )

    return placed


def swap(block, axis, first):
    size = lax.axis_size(axis)
    pairs = [(i, i + 1) for i in range(first, size - 1, 2)]
    return lax.ppermute(block, axis, pairs + [(b, a) for a, b in pairs])


def on_device(
    query_matrix,
    key_matrix,
    value_matrix,
    saved_output,
    output_grad,
    row_logsum,
    key_blocks,
    halo_rows,
):
    queries, keys, values = query_matrix[0], key_matrix[0], value_matrix[0]
    saved, cotangent, logsum = saved_output[0], output_grad[0], row_logsum[0]
    tokens, width = queries.shape
    heads = logsum.shape[0]
    domains, _, cap = halo_rows.shape
    slots = domains * 2 * cap
    me = lax.axis_index("dom").astype(jnp.int32).reshape(1)
    halo = halo_rows.transpose(0, 2, 1)
    array = tokens * width
    packed = 4 * width + LANES

    def exchange(block):
        return lax.all_to_all(
            block.reshape(domains, 2 * cap, width), "dom", split_axis=0, concat_axis=0, tiled=True
        ).reshape(slots, width)

    pack, send = call(
        front_kernel,
        (SMEM,) + (HBM,) * 7,
        (((tokens, packed), BF, VMEM), ((slots, width), BF, HBM)),
        (2 * slots * array, 20 * array),
        (
            (halo.shape, jnp.int32),
            ((tokens, width), BF),
            (logsum.shape, F32),
            ((slots, width), BF),
        ),
        8,
        "front",
    )(me, halo, queries, keys, values, cotangent, saved, logsum)
    first = swap(pack, "hour", 0)
    second = swap(pack, "hour", 1)
    received = exchange(send)
    part, back = call(
        functools.partial(halo_kernel, heads, cap),
        (SMEM, VMEM, VMEM),
        (((3 * tokens, width), F32, HBM), ((slots, width), BF, HBM)),
        (20 * tokens * array, 30 * array),
        (
            ((2 * tokens, width), BF),
            ((3 * tokens, width), F32),
            ((slots, width), BF),
        ),
        heads // 2,
        "halo",
    )(key_blocks.reshape(1), pack, received)
    returned = exchange(back)
    query_grad, total, place = call(
        functools.partial(hours_kernel, heads),
        (SMEM, HBM, VMEM, pl.ANY, pl.ANY, HBM),
        (
            ((tokens, width), BF, HBM),
            ((2 * tokens, width), F32, VMEM),
            ((2 * tokens, slots), BF, VMEM),
        ),
        (56 * tokens * array, 50 * array),
        (
            (halo.shape, jnp.int32),
            ((tokens, packed), BF),
            ((tokens, packed), BF),
            ((3 * tokens, width), F32),
            ((tokens, width), BF),
        ),
        4 + heads // 8,
        "hours",
    )(me, halo, pack, first, second, part)
    key_grad, value_grad = call(
        scatter_kernel,
        (VMEM, VMEM, VMEM),
        (((tokens, width), BF, HBM), ((tokens, width), BF, HBM)),
        (2 * slots * array, 16 * array),
        (((2 * tokens, width), BF),),
        2 * (width // (2 * LANES)),
        "scatter",
    )(place, returned, total)
    return query_grad[None], key_grad[None], value_grad[None]


def solution(mesh):
    in_specs = (
        P("hour", "dom", None),
        P("hour", "dom", None),
        P("hour", "dom", None),
        P("hour", "dom", None),
        P("hour", "dom", None),
        P("hour", None, "dom"),
        P("dom", None),
        P(),
    )
    out_specs = (P("hour", "dom", None), P("hour", "dom", None), P("hour", "dom", None))
    return jax.shard_map(
        on_device, mesh=mesh, in_specs=in_specs, out_specs=out_specs, check_vma=False
    )
```

time: 125 us -> 53.1 us (0.42)
  starting transfers between devices: 51.8 us -> 20.1 us
  local copies, waits for them, and re-layouts: 23.7 us -> 2.19 us
  other arithmetic: 18.4 us -> 0 us
  Pallas kernels: 0 us -> 15.5 us
  matrix products: 8.86 us -> 0 us
  waiting for transfers between devices: 19.1 us -> 13.2 us
    ppermute x8 -> x2, starting transfers between devices: 24.7 us -> 7.91 us  [swap(): return lax.ppermute(block, axis, pairs + [(b, a) for a, b in pairs])]
    pallas_call x0 -> x4, Pallas kernels: none -> 15.5 us  [placed(): run(*(pltpu.with_memory_space_constraint(x, space) if space is HBM else x...]
    all_to_all x4 -> x2, starting transfers between devices: 27 us -> 12.2 us  [exchange(): lax.all_to_all(block.reshape(domains, 2 * cap, width), 'dom', split_axis=...]
    dot_general x5 -> x0, matrix products: 8.86 us -> none  [the longest x1 2.3 us: attend(): jnp.einsum('qhd,khd->hqk', cot_heads, value_heads, preferred_element_type...]
    all_to_all x4 -> x2, waiting for transfers between devices: 19.1 us -> 13.2 us  [exchange(): lax.all_to_all(block.reshape(domains, 2 * cap, width), 'dom', split_axis=...]
    scatter-add x2 -> x0, other arithmetic: 5.42 us -> none  [the longest x1 3.49 us: on_device(): local_dk.at[send_index].add(returned_dk.reshape(-1, feature_width) * weight)]
    ppermute x4 -> x0, local copies, waits for them, and re-layouts: 5.26 us -> none  [from_behind(): return lax.ppermute(block, axis, route)]
    slice x6 -> x0, local copies, waits for them, and re-layouts: 5.18 us -> none  [the longest x1 2.07 us: on_device(): prev_dv_parts = grad_v[split_at:split_at + BLK]]
  transfers between devices with their start and end apart: 12 -> 4, of which waited for: 3 -> 2; matrix products, arithmetic and copies ran while one was open for 32% -> 0% of each run, Pallas kernels for 0% -> 23%
where the time goes in v1:
time: 53.1 us; the launch traced here: 52.3 us
  starting transfers between devices  20.1 us (38%)
  Pallas kernels  15.5 us (29%)
  waiting for transfers between devices  13.2 us (25%)
  local copies, waits for them, and re-layouts  2.19 us (4%)
  between operations  1.36 us (3%)
    pallas_call x4, Pallas kernels, placed(): run(*(pltpu.with_memory_space_constraint(x, space) if space is HBM else x...  15.5 us
    all_to_all x2, waiting for transfers between devices, exchange(): lax.all_to_all(block.reshape(domains, 2 * cap, width), 'dom', split_axis=...  13.2 us
    all_to_all x2, starting transfers between devices, exchange(): lax.all_to_all(block.reshape(domains, 2 * cap, width), 'dom', split_axis=...  12.2 us
    ppermute x2, starting transfers between devices, swap(): return lax.ppermute(block, axis, pairs + [(b, a) for a, b in pairs])  7.91 us
    unnamed x4, local copies, waits for them, and re-layouts  2.19 us
  transfers between devices with their start and end apart: 4, of which 2 were waited for; matrix products, arithmetic and copies ran while one was open for 0% of the time, Pallas kernels for 23%

profile of v1, /device:TPU:1, one launch (start us, length us, event | category | flops | bytes accessed | tf_op | source)
XLA Modules:
  0.0 52.3 jit_solution(14114412750516674966)
XLA Ops:
  0.6 2.3 %front.1 = (bf16[128,4224]{1,0:T(8,128)(2,1)S(1)}, bf16[256,1024]{1,0:T(8,128)(2,1)}) custom-call(s32[1]{0:T(128)} %bitcast.me_ref, s32[32,4,32]{2,1,0:T(4,128)} %bitcast.21, bf16[128,1024]{1,0:T(8,128)(2,1)} %bitcast.23, bf16[128,1024]{1,0:T(8,128)(2,1)} %bitcast.24, bf16[128,1024]{1,0:T(8,128)(2,1)} %bitcast.25, bf16[128,1024]{1,0:T(8,128)(2,1)} %bitcast.26, ...), custom_call_target="tpu_custom_call" | custom-call | flops 67108864 | bytes 2621440 | tf_op jit(solution)/shard_map/front/pallas_call | solution.py:383
  3.0 0.7 %collective-permute-start.1 = (bf16[128,4224]{1,0:T(8,128)(2,1)S(1)}, bf16[128,4224]{1,0:T(8,128)(2,1)S(1)}, u32[]{:S(2)}, u32[]{:S(2)}) collective-permute-start(bf16[128,4224]{1,0:T(8,128)(2,1)S(1)} %get-tuple-element.12.pack_ref), channel_id=1, source_target_pairs={{32,64},{96,128},{160,192},{224,256},{288,320},{352,384},{416,448}... | collective-permute-start | bytes 3244040 | tf_op jit(solution)/shard_map/ppermute | solution.py:396
  3.7 7.2 %collective-permute-start = (bf16[128,4224]{1,0:T(8,128)(2,1)S(1)}, bf16[128,4224]{1,0:T(8,128)(2,1)}, u32[]{:S(2)}, u32[]{:S(2)}) collective-permute-start(bf16[128,4224]{1,0:T(8,128)(2,1)S(1)} %get-tuple-element.12.pack_ref), channel_id=1, source_target_pairs={{0,32},{64,96},{128,160},{192,224},{256,288},{320,352},{384,416},{... | collective-permute-start | bytes 3244040 | tf_op jit(solution)/shard_map/ppermute | solution.py:396
  10.9 8.3 %all-to-all-start = ((bf16[32,8,1024]{2,1,0:T(8,128)(2,1)}), bf16[32,8,1024]{2,1,0:T(8,128)(2,1)S(1)}, u32[]{:S(2)}, u32[]{:S(2)}) async-start(bf16[32,8,1024]{2,1,0:T(8,128)(2,1)} %bitcast.20), calls=%async_computation | async-start | bytes 1048576 | tf_op jit(solution)/shard_map/all_to_all | solution.py:421
  19.9 10.9 %all-to-all-done = bf16[32,8,1024]{2,1,0:T(8,128)(2,1)S(1)} async-done(((bf16[32,8,1024]{2,1,0:T(8,128)(2,1)}), bf16[32,8,1024]{2,1,0:T(8,128)(2,1)S(1)}, u32[]{:S(2)}, u32[]{:S(2)}) %all-to-all-start) | async-done | bytes 524320 | tf_op jit(solution)/shard_map/all_to_all | solution.py:421
  30.9 3.7 %halo.1 = (f32[384,1024]{1,0:T(8,128)}, bf16[256,1024]{1,0:T(8,128)(2,1)}) custom-call(s32[1]{0:T(128)} %bitcast.16.block_ref, bf16[128,4224]{1,0:T(8,128)(2,1)S(1)} %get-tuple-element.12.pack_ref, bf16[256,1024]{1,0:T(8,128)(2,1)S(1)} %bitcast.18), custom_call_target="tpu_custom_call" | custom-call | flops 335544320 | bytes 3932160 | tf_op jit(solution)/shard_map/halo/pallas_call | solution.py:383
  34.5 3.9 %all-to-all-start.1 = ((bf16[32,8,1024]{2,1,0:T(8,128)(2,1)}), bf16[32,8,1024]{2,1,0:T(8,128)(2,1)S(1)}, u32[]{:S(2)}, u32[]{:S(2)}) async-start(bf16[32,8,1024]{2,1,0:T(8,128)(2,1)} %bitcast.19), calls=%async_computation.1 | async-start | bytes 1048576 | tf_op jit(solution)/shard_map/all_to_all | solution.py:421
  38.4 0.0 collective-permute-done.1.second_hbm
  38.4 0.0 collective-permute-done.first_hbm
  38.5 8.4 %hours.1 = (bf16[128,1024]{1,0:T(8,128)(2,1)}, f32[256,1024]{1,0:T(8,128)S(1)}, bf16[256,256]{1,0:T(8,128)(2,1)S(1)}) custom-call(s32[1]{0:T(128)} %bitcast.me_ref, s32[32,4,32]{2,1,0:T(4,128)} %bitcast.22, bf16[128,4224]{1,0:T(8,128)(2,1)S(1)} %get-tuple-element.12.pack_ref, bf16[128,4224]{1,0:T(8,128)(2,1)} %collective-permute-done.first_hbm, ...), custom_call_target="tpu_custom_call" | custom-call | flops 939524096 | bytes 6553600 | tf_op jit(solution)/shard_map/hours/pallas_call | solution.py:383
  46.8 0.0 copy-start
  46.8 1.0 %copy-done = f32[256,1024]{1,0:T(8,128)} copy-done((f32[256,1024]{1,0:T(8,128)}, f32[256,1024]{1,0:T(8,128)S(1)}, u32[]{:S(2)}) %copy-start) | copy-done | bytes 1048600
  47.8 2.2 %all-to-all-done.1 = bf16[32,8,1024]{2,1,0:T(8,128)(2,1)S(1)} async-done(((bf16[32,8,1024]{2,1,0:T(8,128)(2,1)}), bf16[32,8,1024]{2,1,0:T(8,128)(2,1)S(1)}, u32[]{:S(2)}, u32[]{:S(2)}) %all-to-all-start.1) | async-done | bytes 524320 | tf_op jit(solution)/shard_map/all_to_all | solution.py:421
  50.0 0.0 copy-start.1
  50.0 1.2 %copy-done.1 = f32[256,1024]{1,0:T(8,128)S(1)} copy-done((f32[256,1024]{1,0:T(8,128)S(1)}, f32[256,1024]{1,0:T(8,128)}, u32[]{:S(2)}) %copy-start.1) | copy-done | bytes 1048600
  51.3 1.1 %scatter.1 = (bf16[128,1024]{1,0:T(8,128)(2,1)}, bf16[128,1024]{1,0:T(8,128)(2,1)}) custom-call(bf16[256,256]{1,0:T(8,128)(2,1)S(1)} %get-tuple-element.16.place_ref, bf16[256,1024]{1,0:T(8,128)(2,1)S(1)} %bitcast.17, f32[256,1024]{1,0:T(8,128)S(1)} %copy-done.1), custom_call_target="tpu_custom_call" | custom-call | flops 67108864 | bytes 2097152 | tf_op jit(solution)/shard_map/scatter/pallas_call | solution.py:383
Async XLA Ops:
  3.0 35.4 %collective-permute-start.1 = (bf16[128,4224]{1,0:T(8,128)(2,1)S(1)}, bf16[128,4224]{1,0:T(8,128)(2,1)S(1)}, u32[]{:S(2)}, u32[]{:S(2)}) collective-permute-start(bf16[128,4224]{1,0:T(8,128)(2,1)S(1)} %get-tuple-element.12.pack_ref), channel_id=1, source_target_pairs={{32,64},{96,128},{160,192},{224,256},{288,320},{352,384},{416,448}... | collective-permute-start | bytes 3244040 | tf_op jit(solution)/shard_map/ppermute | solution.py:396
  3.7 34.7 %collective-permute-start = (bf16[128,4224]{1,0:T(8,128)(2,1)S(1)}, bf16[128,4224]{1,0:T(8,128)(2,1)}, u32[]{:S(2)}, u32[]{:S(2)}) collective-permute-start(bf16[128,4224]{1,0:T(8,128)(2,1)S(1)} %get-tuple-element.12.pack_ref), channel_id=1, source_target_pairs={{0,32},{64,96},{128,160},{192,224},{256,288},{320,352},{384,416},{... | collective-permute-start | bytes 3244040 | tf_op jit(solution)/shard_map/ppermute | solution.py:396
  10.9 19.9 %all-to-all-start = ((bf16[32,8,1024]{2,1,0:T(8,128)(2,1)}), bf16[32,8,1024]{2,1,0:T(8,128)(2,1)S(1)}, u32[]{:S(2)}, u32[]{:S(2)}) async-start(bf16[32,8,1024]{2,1,0:T(8,128)(2,1)} %bitcast.20), calls=%async_computation | async-start | bytes 1048576 | tf_op jit(solution)/shard_map/all_to_all | solution.py:421
  34.5 15.5 %all-to-all-start.1 = ((bf16[32,8,1024]{2,1,0:T(8,128)(2,1)}), bf16[32,8,1024]{2,1,0:T(8,128)(2,1)S(1)}, u32[]{:S(2)}, u32[]{:S(2)}) async-start(bf16[32,8,1024]{2,1,0:T(8,128)(2,1)} %bitcast.19), calls=%async_computation.1 | async-start | bytes 1048576 | tf_op jit(solution)/shard_map/all_to_all | solution.py:421
  46.8 1.0 %copy-start = (f32[256,1024]{1,0:T(8,128)}, f32[256,1024]{1,0:T(8,128)S(1)}, u32[]{:S(2)}) copy-start(f32[256,1024]{1,0:T(8,128)S(1)} %get-tuple-element.18.total_ref) | copy-start | bytes 3145732
  50.0 1.2 %copy-start.1 = (f32[256,1024]{1,0:T(8,128)S(1)}, f32[256,1024]{1,0:T(8,128)}, u32[]{:S(2)}) copy-start(f32[256,1024]{1,0:T(8,128)} %copy-done) | copy-start | bytes 3145732
